TPU v7x, 512 devices: a whole 4x8x8 slice. The times are simulated.
512 devices in a mesh: prow: 16 (over x, z_hi), pcol: 32 (over z_lo, y, core).
Axes of the slice: x: 4, y: 8, z: 8 (z_hi: 4, z_lo: 2; z = z_hi * 2 + z_lo), core: 2. Of those that a mesh axis runs over, the one named last changes fastest.
Arguments:
- ancestor_inverse: bfloat16 [24576, 24576], P('pcol', 'prow'), may hold values from -6 to 6
- lower_panel: bfloat16 [24576, 1024], P(('prow', 'pcol')), may hold values from -0.3125 to 0.3125
- pivot_inverse: float32 [256, 1024], P('pcol', 'prow'), may hold values from -6 to 6
- struct_list: int32 [4, 48], replicated, may hold values from -1 to 95, as said below
Outputs:
- off_inverse: bfloat16 [24576, 1024], P('pcol', 'prow')
- diag_inverse: float32 [256, 1024], P('pcol', 'prow')
Inputs may be any that keep to these rules, and one draw needn't show every extreme that they name: `struct_list`: each row lists distinct ancestor supernodes first, all within 48 cyclically consecutive ancestor numbers, then entries -1; every row has at least one ancestor and some row lists 48.
All inputs are finite; a program needn't handle non-finite values.
Results may differ from a plain program's by a relative error of at most 0.001.
Values may be sent and summed in bfloat16 or wider, within the bound.
A program may use at most 64 MiB of HBM per device.

v0:
```python
import jax
import jax.numpy as jnp
from jax import lax
from jax.sharding import PartitionSpec as P

B = 256
NK = 4


def from_root(value, axis, root):
    mine = lax.axis_index(axis) == root
    return lax.psum(jnp.where(mine, value, jnp.zeros_like(value)), axis)


def membership(struct_list, ancestor_ids):
    listed = struct_list[:, :, None] == ancestor_ids[None, None, :]
    return jnp.transpose(jnp.any(listed, axis=1))


def body(ancestor_inverse, lower_panel, pivot_inverse, struct_list):
    row_count = ancestor_inverse.shape[0] // B
    col_count = ancestor_inverse.shape[1] // B
    grid_rows = lax.axis_size("prow")
    prow_index = lax.axis_index("prow")
    pcol_index = lax.axis_index("pcol")
    col_share = NK * B // grid_rows
    gathered = lax.all_gather(lower_panel, "pcol", axis=0, tiled=True)
    col_ids = prow_index * col_count + jnp.arange(col_count, dtype=jnp.int32)
    row_ids = pcol_index * row_count + jnp.arange(row_count, dtype=jnp.int32)
    member_cols = membership(struct_list, col_ids)
    member_rows = membership(struct_list, row_ids)
    scaled = gathered.reshape(col_count, B, NK, B) * member_cols[:, None, :, None].astype(
        jnp.bfloat16
    )
    masked = scaled.reshape(col_count * B, NK * B)
    partial_value = -jnp.dot(ancestor_inverse, masked, preferred_element_type=jnp.float32)
    share_sum = lax.psum_scatter(partial_value, "prow", scatter_dimension=1, tiled=True)
    columns = prow_index * col_share + jnp.arange(col_share, dtype=jnp.int32)
    block_of = columns // B
    one_hot = block_of[:, None] == jnp.arange(NK, dtype=jnp.int32)[None, :]
    row_mask = jnp.any(member_rows[:, None, :] & one_hot[None, :, :], axis=2).astype(jnp.float32)
    off_share = (share_sum.reshape(row_count, B, col_share) * row_mask[:, None, :]).reshape(
        row_count * B, col_share
    )
    off_inverse = off_share.astype(jnp.bfloat16)
    block_count = max(col_share // B, 1)
    column_width = col_share // block_count
    offset_blocks = pcol_index * row_count % col_count
    root_row = pcol_index * row_count // col_count
    piece = lax.dynamic_slice_in_dim(masked, offset_blocks * B, row_count * B, 0)
    lower_rows = from_root(piece, "prow", root_row)
    first_block = prow_index * col_share // B
    lower_slice = lax.dynamic_slice_in_dim(lower_rows, first_block * B, block_count * B, 1)
    lower_blocks = lower_slice.astype(jnp.float32).reshape(row_count * B, block_count, B)
    off_blocks = off_share.reshape(row_count * B, block_count, column_width)
    diag_term = jnp.einsum(
        "ikr,ikc->rkc", lower_blocks, off_blocks, precision=lax.Precision.HIGHEST
    ).reshape(B, col_share)
    diag_share = lax.psum_scatter(diag_term, "pcol", scatter_dimension=0, tiled=True)
    diag_inverse = pivot_inverse - diag_share
    return (off_inverse, diag_inverse)


def solution(mesh):
    placed = (P("pcol", "prow"), P(("prow", "pcol"), None), P("pcol", "prow"), P())
    return jax.shard_map(
        body,
        mesh=mesh,
        in_specs=placed,
        out_specs=(P("pcol", "prow"), P("pcol", "prow")),
        check_vma=False,
    )
```

profile of v0, /device:TPU:1, one launch (start us, length us, event | category | flops | bytes accessed | tf_op | source)
XLA Modules:
  0.0 579.8 jit_solution(7268216275840129706)
XLA Ops:
  7.2 0.0 copy-start
  7.2 0.0 all-gather.2.cloned.1.call-start
  7.2 0.7 all-gather.2.cloned.1.call-update
  7.9 0.0 all-reduce.4.cloned.1.call-start
  8.0 0.9 compare_reduce_fusion
  8.9 0.9 mul.43
  9.8 2.5 copy.20
  12.3 72.4 %all-gather.2.cloned.1.call-done = bf16[1536,1024]{1,0:T(8,128)(2,1)} async-done(((bf16[48,1024]{1,0:T(8,128)(2,1)}), bf16[1536,1024]{1,0:T(8,128)(2,1)}) %all-gather.2.cloned.1.call-update) | async-done | bytes 3145744 | tf_op jit(solution)/shard_map/all_gather | solution.py:27
  84.7 4.4 mul.45
  89.0 0.0 copy-start.1
  89.0 1.7 copy-done.1
  90.7 1.6 dynamic-slice_select_fusion
  92.3 0.0 all-reduce.4.cloned.1.call-update
  92.3 0.0 reduce-scatter.3.cloned.1.call-start
  92.4 6.3 %negate_bitcast_fusion = f32[768,1024]{0,1:T(8,128)} fusion(bf16[1536,1024]{1,0:T(8,128)(2,1)} %copy-done.1, bf16[768,1536]{1,0:T(8,128)(2,1)S(1)} %copy-done), kind=kOutput, calls=%fused_computation | convolution fusion | flops 2416705536 | bytes 8650752 | tf_op jit(solution)/shard_map/dot_general | solution.py:36
  98.7 0.0 reduce-scatter.3.cloned.1.call-update
  98.7 0.0 all-reduce.6.cloned.1.call-start
  98.8 0.6 copy-done.2
  99.3 0.2 compare_reduce_fusion.1
  99.6 0.1 and_reduce_fusion
  99.7 0.1 copy.15
  99.8 0.1 mul.48
  100.0 0.1 copy.16
  100.0 1.3 dynamic-slice
  102.0 160.1 %all-reduce.4.cloned.1.call-done = bf16[768,1024]{1,0:T(8,128)(2,1)} async-done(((bf16[768,1024]{1,0:T(8,128)(2,1)}), bf16[768,1024]{1,0:T(8,128)(2,1)}) %all-reduce.4.cloned.1.call-update) | async-done | bytes 1572880 | tf_op jit(solution)/shard_map/psum | solution.py:12
  262.0 108.7 %reduce-scatter.3.cloned.1.call-done = f32[768,64]{0,1:T(8,128)} async-done(((f32[768,1024]{0,1:T(8,128)}), f32[768,64]{0,1:T(8,128)}) %reduce-scatter.3.cloned.1.call-update) | async-done | bytes 196624 | tf_op jit(solution)/shard_map/reduce_scatter | solution.py:37
  370.7 2.0 convolution_bitcast_fusion
  372.7 0.0 all-reduce.6.cloned.1.call-update
  372.8 1.6 multiply_convert_fusion
  374.4 197.4 %all-reduce.6.cloned.1.call-done = f32[256,64]{0,1:T(8,128)} async-done(((f32[256,64]{0,1:T(8,128)}), f32[256,64]{0,1:T(8,128)}) %all-reduce.6.cloned.1.call-update) | async-done | bytes 65552
  571.7 0.8 dynamic-slice_subtract_fusion
  572.6 0.7 copy.17
  (11 shorter events, 0.1 us)
Async XLA Ops:
  7.2 85.2 %copy-start = (bf16[768,1536]{1,0:T(8,128)(2,1)S(1)}, bf16[768,1536]{1,0:T(8,128)(2,1)}, u32[]{:S(2)}) copy-start(bf16[768,1536]{1,0:T(8,128)(2,1)} %param.4) | copy-start | bytes 7077892
  7.2 77.5 %all-gather.2.cloned.1.call-start = ((), (), s32[]{:S(2)}) async-start(), calls=%async_computation.1 | async-start | bytes 3244032 | tf_op jit(solution)/shard_map/all_gather | solution.py:27
  7.9 254.1 %all-reduce.4.cloned.1.call-start = ((), (), s32[]{:S(2)}) async-start(), calls=%async_computation.3 | async-start | bytes 3145728 | tf_op jit(solution)/shard_map/psum | solution.py:12
  89.0 1.7 copy-start.1
  92.3 278.3 %reduce-scatter.3.cloned.1.call-start = ((), (), s32[]{:S(2)}) async-start(), calls=%async_computation.2 | async-start | bytes 3342336 | tf_op jit(solution)/shard_map/reduce_scatter | solution.py:37
  98.7 0.7 copy-start.2
  98.7 1.3 copy-start.3
  98.7 473.0 %all-reduce.6.cloned.1.call-start = ((), (), s32[]{:S(2)}) async-start(), calls=%async_computation.4 | async-start | bytes 131072
Sparse Core Ops, SparseCore 0:
  10.1 74.4 all-gather.1
  92.5 169.5 all-reduce.3
  266.2 104.4 reduce-scatter.2
  373.5 198.2 all-reduce.5
where the time goes:
time: 581 us; the launch traced here: 580 us
  waiting for transfers between devices  539 us (93%)
  between operations  14.6 us (3%)
  other arithmetic  9.68 us (2%)
  matrix products  8.3 us (1%)
  local copies, waits for them, and re-layouts  7.86 us (1%)
    unnamed x5, waiting for transfers between devices  198 us
    psum x1, waiting for transfers between devices, from_root(): return lax.psum(jnp.where(mine, value, jnp.zeros_like(value)), axis)  160 us
    reduce_scatter x1, waiting for transfers between devices, body(): lax.psum_scatter(partial_value, 'prow', scatter_dimension=1, tiled=True)  109 us
    all_gather x1, waiting for transfers between devices, body(): gathered = lax.all_gather(lower_panel, 'pcol', axis=0, tiled=True)  72.4 us
  transfers between devices with their start and end apart: 4, of which 4 were waited for; matrix products, arithmetic and copies ran while one was open for 2% of the time, Pallas kernels for 0%

commit v1 on v0

v1 whole, which is shorter than its diff:
```python
import jax
import jax.numpy as jnp
from jax import lax
from jax.experimental import pallas as pl
from jax.experimental.pallas import tpu as pltpu
from jax.sharding import PartitionSpec as P

B = 256
NK = 4
MESH = pl.DeviceIdType.MESH
F32 = jnp.float32
BF16 = jnp.bfloat16
ROWS = 48
SHARES = 16


def remote(src, dst, send, recv, device):
    return pltpu.make_async_remote_copy(
        src_ref=src, dst_ref=dst, send_sem=send, recv_sem=recv, device_id=device, device_id_type=MESH
    )


def kernel(
    mask,
    inverse,
    lower,
    pivot,
    off_out,
    diag_out,
    gathered,
    masked,
    own_rows,
    part,
    x_in,
    z_part,
    z_in,
    diag_part,
    diag_in,
    local_sem,
    pair_sem,
    ring_send,
    ring_recv,
    core_send,
    core_recv,
    rows_send,
    rows_recv,
    x_send,
    x_recv,
    z_send,
    z_recv,
    diag_send,
    diag_recv,
):
    r, c = lax.axis_index("prow"), lax.axis_index("pcol")
    x, zh = r // 4, r % 4
    zl, y, core = c // 16, (c % 16) // 2, c % 2
    target_col = 2 * r + c // SHARES
    slot = c % SHARES
    source_row = c // 2
    source_col = (c % 2) * SHARES
    self_rows = target_col == c

    def col_device(z_lo, y_at, core_at):
        return {"prow": r, "pcol": z_lo * 16 + y_at * 2 + core_at}

    def x_device(step):
        return {"prow": ((x + step + 4) % 4) * 4 + zh, "pcol": c}

    def z_device(step):
        return {"prow": x * 4 + (zh + step + 4) % 4, "pcol": c}

    barrier = pltpu.get_barrier_semaphore()

    @pl.loop(1, 32)
    def _(i):
        pl.semaphore_signal(
            barrier, inc=1, device_id={"prow": r, "pcol": (c + i) % 32}, device_id_type=MESH
        )

    for device in (x_device(1), x_device(-1), z_device(1), z_device(-1)):
        pl.semaphore_signal(barrier, inc=1, device_id=device, device_id_type=MESH)

    @pl.loop(0, SHARES)
    def _(s):
        @pl.when(jnp.logical_not((source_row == r) & (source_col + s == c)))
        def _():
            pl.semaphore_signal(
                barrier,
                inc=1,
                device_id={"prow": source_row, "pcol": source_col + s},
                device_id_type=MESH,
            )

    pl.semaphore_wait(barrier, 35 + SHARES - self_rows.astype(jnp.int32))

    def shard(z_lo, y_at, core_at):
        at = (z_lo * 16 + y_at * 2 + core_at) * ROWS
        return gathered.at[pl.ds(pl.multiple_of(at, 16), ROWS)]

    sent = []
    core_copies = []

    def to_core(src, dst):
        n = len(core_copies)
        copy = remote(src, dst, core_send.at[n], core_recv.at[n], col_device(zl, y, 1 - core))
        copy.start()
        core_copies.append(copy)

    ring = {}

    def to_ring(chain, way, step, src, dst):
        n = (chain * 2 + way) * 4 + step
        device = col_device(zl, (y + (1 if way == 0 else 7)) % 8, core)
        copy = remote(src, dst, ring_send.at[n], ring_recv.at[n], device)
        copy.start()
        ring[chain, way, step] = copy

    mine = shard(zl, y, core)
    pair = remote(lower, mine, pair_sem.at[0], pair_sem.at[1], col_device(1 - zl, y, core))
    pair.start()
    to_ring(0, 0, 0, lower, mine)
    to_ring(0, 1, 0, lower, mine)
    to_core(lower, mine)
    keep = pltpu.make_async_copy(lower, mine, local_sem)
    keep.start()
    pair.wait_recv()
    theirs = shard(1 - zl, y, core)
    to_ring(1, 0, 0, theirs, theirs)
    to_ring(1, 1, 0, theirs, theirs)
    to_core(theirs, theirs)
    for step in range(1, 5):
        for chain in range(2):
            for way in range(2):
                if (chain, way, step - 1) not in ring:
                    continue
                ring[chain, way, step - 1].wait_recv()
                origin = (y + (8 - step if way == 0 else step)) % 8
                piece = shard(zl if chain == 0 else 1 - zl, origin, core)
                if step < 3 or (step == 3 and chain == way):
                    to_ring(chain, way, step, piece, piece)
                to_core(piece, piece)

    def rows_copy(i):
        row = (r + i) % 16
        columns = pl.ds(pl.multiple_of((row // 4) * B, B), B)
        return remote(
            lower.at[:, columns],
            own_rows.at[pl.ds(pl.multiple_of(slot * ROWS, 16), ROWS)],
            rows_send.at[i],
            rows_recv.at[slot],
            {"prow": row, "pcol": target_col},
        )

    @pl.loop(1, 16)
    def _(i):
        rows_copy(i).start()

    @pl.when(jnp.logical_not(self_rows))
    def _():
        rows_copy(0).start()

    @pl.when(self_rows)
    def _():
        columns = pl.ds(pl.multiple_of(x * B, B), B)
        own_rows[pl.ds(pl.multiple_of(slot * ROWS, 16), ROWS), :] = lower[:, columns]

    keep.wait()
    for copy in core_copies:
        copy.wait_recv()

    @pl.loop(0, 6)
    def _(j):
        rows = pl.ds(pl.multiple_of(j * B, B), B)
        for k in range(NK):
            columns = pl.ds(k * B, B)
            value = gathered[rows, columns].astype(F32) * mask[j * NK + k]
            masked[rows, columns] = value.astype(BF16)

    def multiply(k):
        columns = pl.ds(pl.multiple_of(k * B, B), B)

        @pl.loop(0, 2)
        def _(half):
            rows = pl.ds(pl.multiple_of(half * 384, 128), 384)
            part[k, half] = jnp.dot(
                inverse[rows, :], masked[:, columns], preferred_element_type=F32
            )

    def hop(source, target, n, sends, recvs, device):
        copy = remote(source, target.at[n], sends.at[n], recvs.at[n], device)
        copy.start()
        sent.append(copy)
        return copy

    far, ahead, behind = (x + 2) % 4, (x + 1) % 4, (x + 3) % 4
    multiply(far)
    mid_up = hop(part.at[far, 0], x_in, 0, x_send, x_recv, x_device(1))
    mid_down = hop(part.at[far, 1], x_in, 1, x_send, x_recv, x_device(-1))
    multiply(ahead)
    raw_up = hop(part.at[ahead, 1], x_in, 2, x_send, x_recv, x_device(1))
    multiply(behind)
    raw_down = hop(part.at[behind, 0], x_in, 4, x_send, x_recv, x_device(-1))
    multiply(x)
    mid_up.wait_recv()
    part[ahead, 0] = part[ahead, 0] + x_in[0]
    sum_up = hop(part.at[ahead, 0], x_in, 3, x_send, x_recv, x_device(1))
    mid_down.wait_recv()
    part[behind, 1] = part[behind, 1] + x_in[1]
    sum_down = hop(part.at[behind, 1], x_in, 5, x_send, x_recv, x_device(-1))
    raw_up.wait_recv()
    raw_down.wait_recv()
    part[x, 0] = part[x, 0] + x_in[4]
    part[x, 1] = part[x, 1] + x_in[2]
    sum_up.wait_recv()
    sum_down.wait_recv()

    for h in range(4):
        lanes = slice(64 * h, 64 * h + 64)
        for half in range(2):
            rows = pl.ds(half * 192, 192)
            low = part[x, 0, rows, lanes] + x_in[3, rows, lanes]
            high = part[x, 1, rows, lanes] + x_in[5, rows, lanes]
            z_part[h, half] = jnp.concatenate([low, high], axis=1)

    far, ahead, behind = (zh + 2) % 4, (zh + 1) % 4, (zh + 3) % 4
    mid_up = hop(z_part.at[far, 0], z_in, 0, z_send, z_recv, z_device(1))
    mid_down = hop(z_part.at[far, 1], z_in, 1, z_send, z_recv, z_device(-1))
    raw_up = hop(z_part.at[ahead, 1], z_in, 2, z_send, z_recv, z_device(1))
    raw_down = hop(z_part.at[behind, 0], z_in, 4, z_send, z_recv, z_device(-1))
    mid_up.wait_recv()
    z_part[ahead, 0] = z_part[ahead, 0] + z_in[0]
    sum_up = hop(z_part.at[ahead, 0], z_in, 3, z_send, z_recv, z_device(1))
    mid_down.wait_recv()
    z_part[behind, 1] = z_part[behind, 1] + z_in[1]
    sum_down = hop(z_part.at[behind, 1], z_in, 5, z_send, z_recv, z_device(-1))

    @pl.loop(0, SHARES)
    def _(s):
        @pl.when(jnp.logical_not((source_row == r) & (source_col + s == c)))
        def _():
            here = own_rows.at[pl.ds(pl.multiple_of(s * ROWS, 16), ROWS)]
            remote(here, here, rows_send.at[0], rows_recv.at[s], x_device(1)).wait_recv()

    raw_up.wait_recv()
    raw_down.wait_recv()
    sum_up.wait_recv()
    sum_down.wait_recv()
    lane = lax.broadcasted_iota(jnp.int32, (192, 128), 1)
    row = lax.broadcasted_iota(jnp.int32, (192, 128), 0) + jnp.where(lane < 64, 0, 384)
    upper = jnp.zeros((B, 128), F32)
    lower_half = jnp.zeros((B, 128), F32)
    for half in range(2):
        at = row + half * 192
        keep_row = jnp.where(at < B, mask[24], jnp.where(at < 2 * B, mask[25], mask[26]))
        first, second = (3, 4) if half == 0 else (5, 2)
        total = (z_part[zh, half] + z_in[first] + z_in[second]) * keep_row
        off_out[pl.ds(half * 192, 192), :] = total[:, :64].astype(BF16)
        off_out[pl.ds(384 + half * 192, 192), :] = total[:, 64:].astype(BF16)
        big = total.astype(BF16)
        small = (total - big.astype(F32)).astype(BF16)
        left = own_rows[pl.ds(half * 192, 192), :]
        right = own_rows[pl.ds(384 + half * 192, 192), :]
        over_rows = (((0,), (0,)), ((), ()))
        for piece in (big, small):
            upper = upper + lax.dot_general(left, piece, over_rows, preferred_element_type=F32)
            lower_half = lower_half + lax.dot_general(
                right, piece, over_rows, preferred_element_type=F32
            )
    lane = lax.broadcasted_iota(jnp.int32, (B, 128), 1)
    diag_part[...] = jnp.where(lane < 64, upper, lower_half)

    def diag_copy(i):
        to = (c + i) % 32
        return remote(
            diag_part.at[pl.ds(pl.multiple_of(to * 8, 8), 8)],
            diag_in.at[c],
            diag_send.at[i],
            diag_recv.at[c],
            {"prow": r, "pcol": to},
        )

    @pl.loop(1, 32)
    def _(i):
        diag_copy(i).start()

    diag_in[c] = diag_part[pl.ds(pl.multiple_of(c * 8, 8), 8), :]

    pair.wait_send()
    for copy in list(ring.values()) + core_copies + sent:
        copy.wait_send()

    @pl.loop(1, 16)
    def _(i):
        rows_copy(i).wait_send()

    @pl.when(jnp.logical_not(self_rows))
    def _():
        rows_copy(0).wait_send()

    @pl.loop(1, 32)
    def _(i):
        diag_copy(i).wait_send()
        source = (c + i) % 32
        here = diag_in.at[source]
        remote(here, here, diag_send.at[0], diag_recv.at[source], x_device(1)).wait_recv()

    term = jnp.sum(diag_in[...], axis=0)
    diag_out[...] = pivot[...] - (term[:, :64] + term[:, 64:])


def body(ancestor_inverse, lower_panel, pivot_inverse, struct_list):
    r, c = lax.axis_index("prow"), lax.axis_index("pcol")
    col_ids = r * 6 + jnp.arange(6, dtype=jnp.int32)
    row_ids = c * 3 + jnp.arange(3, dtype=jnp.int32)
    cols = jnp.any(struct_list[None, :, :] == col_ids[:, None, None], axis=2)
    level = lax.dynamic_slice_in_dim(struct_list, r // 4, 1, 0)
    rows = jnp.any(level == row_ids[:, None], axis=1)
    mask = jnp.concatenate(
        [-cols.astype(F32).reshape(24), rows.astype(F32), jnp.zeros((5,), F32)]
    )
    vmem = pl.BlockSpec(memory_space=pltpu.VMEM)
    dma = pltpu.SemaphoreType.DMA
    return pl.pallas_call(
        kernel,
        out_shape=(
            jax.ShapeDtypeStruct((768, 64), BF16),
            jax.ShapeDtypeStruct((8, 64), F32),
        ),
        in_specs=[pl.BlockSpec(memory_space=pltpu.SMEM), vmem, vmem, vmem],
        out_specs=(vmem, vmem),
        scratch_shapes=[
            pltpu.VMEM((1536, 1024), BF16),
            pltpu.VMEM((1536, 1024), BF16),
            pltpu.VMEM((768, B), BF16),
            pltpu.VMEM((4, 2, 384, B), F32),
            pltpu.VMEM((6, 384, B), F32),
            pltpu.VMEM((4, 2, 192, 128), F32),
            pltpu.VMEM((6, 192, 128), F32),
            pltpu.VMEM((B, 128), F32),
            pltpu.VMEM((32, 8, 128), F32),
            dma,
            dma((2,)),
            dma((16,)),
            dma((16,)),
            dma((16,)),
            dma((16,)),
            dma((16,)),
            dma((16,)),
            dma((6,)),
            dma((6,)),
            dma((6,)),
            dma((6,)),
            dma((32,)),
            dma((32,)),
        ],
        compiler_params=pltpu.CompilerParams(
            collective_id=0, has_side_effects=True, vmem_limit_bytes=48 * 1024 * 1024
        ),
    )(mask, ancestor_inverse, lower_panel, pivot_inverse)


def solution(mesh):
    placed = (P("pcol", "prow"), P(("prow", "pcol"), None), P("pcol", "prow"), P())
    return jax.shard_map(
        body,
        mesh=mesh,
        in_specs=placed,
        out_specs=(P("pcol", "prow"), P("pcol", "prow")),
        check_vma=False,
    )
```

time: 581 us -> 152 us (0.26)
  waiting for transfers between devices: 539 us -> 0 us
  Pallas kernels: 0 us -> 145 us
  between operations: 14.6 us -> 0.67 us
  other arithmetic: 9.68 us -> 1.22 us
  matrix products: 8.3 us -> 0 us
    unnamed x5 -> x0, waiting for transfers between devices: 198 us -> none
    psum x1 -> x0, waiting for transfers between devices: 160 us -> none  [from_root(): return lax.psum(jnp.where(mine, value, jnp.zeros_like(value)), axis)]
    pallas_call x0 -> x1, Pallas kernels: none -> 145 us  [body(): pl.pallas_call(kernel, out_shape=(jax.ShapeDtypeStruct((768, 64), BF16),...]
    reduce_scatter x1 -> x0, waiting for transfers between devices: 109 us -> none  [body(): lax.psum_scatter(partial_value, 'prow', scatter_dimension=1, tiled=True)]
    all_gather x1 -> x0, waiting for transfers between devices: 72.4 us -> none  [body(): gathered = lax.all_gather(lower_panel, 'pcol', axis=0, tiled=True)]
    dot_general x2 -> x0, matrix products: 8.3 us -> none  [the longest x1 6.25 us: body(): jnp.dot(ancestor_inverse, masked, preferred_element_type=jnp.float32)]
  transfers between devices with their start and end apart: 4 -> 0, of which waited for: 4 -> 0; matrix products, arithmetic and copies ran while one was open for 2% -> 0% of each run, Pallas kernels for 0% -> 0%
where the time goes in v1:
time: 152 us
  Pallas kernels  145 us (95%)
  local copies, waits for them, and re-layouts  5.39 us (4%)
    pallas_call x1, Pallas kernels, body(): pl.pallas_call(kernel, out_shape=(jax.ShapeDtypeStruct((768, 64), BF16),...  145 us
    unnamed x7, local copies, waits for them, and re-layouts  3.84 us

profile of v1, /device:TPU:1, one launch (start us, length us, event | category | flops | bytes accessed | tf_op | source)
XLA Modules:
  0.0 152.1 jit_solution(15931840305223825428)
XLA Ops:
  0.6 0.7 dynamic-slice_bitcast_fusion
  1.3 0.2 compare_reduce_fusion.1
  1.5 0.9 compare_reduce_fusion
  2.5 0.1 neg.7
  2.6 0.1 pad_maximum_fusion.mask
  2.6 0.0 copy-start
  2.7 1.7 %copy-done = bf16[768,1536]{1,0:T(8,128)(2,1)S(1)} copy-done((bf16[768,1536]{1,0:T(8,128)(2,1)S(1)}, bf16[768,1536]{1,0:T(8,128)(2,1)}, u32[]{:S(2)}) %copy-start) | copy-done | bytes 2359320
  4.3 0.0 copy-start.1
  4.3 0.9 copy-done.1
  5.2 0.0 copy-start.2
  5.2 0.7 copy-done.2
  5.9 144.8 %shard_map.59 = (bf16[768,64]{1,0:T(8,128)(2,1)S(1)}, f32[8,64]{1,0:T(8,128)S(1)}) custom-call(f32[32]{0:T(128)S(1)} %pad_maximum_fusion.mask, bf16[768,1536]{1,0:T(8,128)(2,1)S(1)} %copy-done, bf16[48,1024]{1,0:T(8,128)(2,1)S(1)} %copy-done.1, f32[8,64]{1,0:T(8,128)S(1)} %copy-done.2), custom_call_target="tpu_custom_call" | custom-call | tf_op jit(solution)/shard_map/pallas_call | solution.py:323
  150.7 0.8 copy.8
  151.5 0.6 copy.10
  (5 shorter events, 0.0 us)
Async XLA Ops:
  2.6 1.7 %copy-start = (bf16[768,1536]{1,0:T(8,128)(2,1)S(1)}, bf16[768,1536]{1,0:T(8,128)(2,1)}, u32[]{:S(2)}) copy-start(bf16[768,1536]{1,0:T(8,128)(2,1)} %inverse.1) | copy-start | bytes 7077892
  4.3 0.9 copy-start.1
  5.2 0.7 copy-start.2

commit v2 on v0

v2 whole, which is shorter than its diff:
```python
import jax
import jax.numpy as jnp
from jax import lax
from jax.experimental import pallas as pl
from jax.experimental.pallas import tpu as pltpu
from jax.sharding import PartitionSpec as P

B = 256
NK = 4
MESH = pl.DeviceIdType.MESH
F32 = jnp.float32
BF16 = jnp.bfloat16
ROWS = 48
SHARES = 16
CHUNKS = 2
CHUNK = 384 // CHUNKS


def remote(src, dst, send, recv, device):
    return pltpu.make_async_remote_copy(
        src_ref=src, dst_ref=dst, send_sem=send, recv_sem=recv, device_id=device, device_id_type=MESH
    )


def kernel(
    lists,
    inverse_hbm,
    lower,
    pivot_hbm,
    off_out,
    diag_out,
    inverse,
    pivot,
    gathered,
    masked,
    row_in,
    own_rows,
    part,
    x_in,
    z_part,
    z_in,
    core_part,
    core_in,
    pair_part,
    pair_in,
    y_part,
    y_in,
    local_sem,
    pair_sem,
    ring_send,
    ring_recv,
    core_send,
    core_recv,
    row_sem,
    slice_send,
    slice_recv,
    band_send,
    band_recv,
    x_send,
    x_recv,
    z_send,
    z_recv,
    sum_sem,
    y_send,
    y_recv,
):
    r, c = lax.axis_index("prow"), lax.axis_index("pcol")
    x, zh = r // 4, r % 4
    zl, y, core = c // 16, (c % 16) // 2, c % 2
    share = zh * 4 + x
    source = {"prow": c // 2, "pcol": (c % 2) * SHARES + share}
    target_row, target_col = (c % 4) * 4 + (c % SHARES) // 4, 2 * r + c // SHARES
    stays = (target_row == r) & (target_col == c)

    def col_device(z_lo, y_at, core_at):
        return {"prow": r, "pcol": z_lo * 16 + (y_at % 8) * 2 + core_at}

    def x_device(step):
        return {"prow": ((x + step + 4) % 4) * 4 + zh, "pcol": c}

    def z_device(step):
        return {"prow": x * 4 + (zh + step + 4) % 4, "pcol": c}

    big_copy = pltpu.make_async_copy(inverse_hbm, inverse, local_sem.at[1])
    big_copy.start()
    pivot_copy = pltpu.make_async_copy(pivot_hbm, pivot, local_sem.at[2])
    pivot_copy.start()

    barrier = pltpu.get_barrier_semaphore()
    friends = [col_device(zl, y + i, core) for i in range(1, 8)]
    friends += [col_device(zl, y, 1 - core), col_device(1 - zl, y, core)]
    friends += [x_device(1), x_device(2), x_device(3), z_device(1), z_device(-1)]
    for device in friends:
        pl.semaphore_signal(barrier, inc=1, device_id=device, device_id_type=MESH)

    @pl.when(jnp.logical_not(stays))
    def _():
        pl.semaphore_signal(barrier, inc=1, device_id=source, device_id_type=MESH)

    pl.semaphore_wait(barrier, len(friends) + 1 - stays.astype(jnp.int32))

    def shard(z_lo, y_at, core_at):
        at = (z_lo * 16 + y_at * 2 + core_at) * ROWS
        return gathered.at[pl.ds(pl.multiple_of(at, 16), ROWS)]

    sent = []
    core_copies = []

    def send(src, dst, send_sem, recv_sem, device):
        copy = remote(src, dst, send_sem, recv_sem, device)
        copy.start()
        sent.append(copy)
        return copy

    def to_core(src, dst):
        n = len(core_copies)
        core_copies.append(
            send(src, dst, core_send.at[n], core_recv.at[n], col_device(zl, y, 1 - core))
        )

    ring = {}

    def to_ring(chain, way, step, src, dst):
        n = (chain * 2 + way) * 4 + step
        device = col_device(zl, y + (1 if way == 0 else 7), core)
        ring[chain, way, step] = send(src, dst, ring_send.at[n], ring_recv.at[n], device)

    mine = shard(zl, y, core)
    pair = send(lower, mine, pair_sem.at[0], pair_sem.at[1], col_device(1 - zl, y, core))
    to_ring(0, 0, 0, lower, mine)
    to_ring(0, 1, 0, lower, mine)
    to_core(lower, mine)
    keep = pltpu.make_async_copy(lower, mine, local_sem.at[0])
    keep.start()
    row_copy = remote(
        lower, row_in, row_sem.at[0], row_sem.at[1], {"prow": target_row, "pcol": target_col}
    )
    row_keep = pltpu.make_async_copy(lower, row_in, row_sem.at[2])

    @pl.when(jnp.logical_not(stays))
    def _():
        row_copy.start()

    @pl.when(stays)
    def _():
        row_keep.start()

    pair.wait_recv()
    theirs = shard(1 - zl, y, core)
    to_ring(1, 0, 0, theirs, theirs)
    to_ring(1, 1, 0, theirs, theirs)
    to_core(theirs, theirs)
    for step in range(1, 5):
        for chain in range(2):
            for way in range(2):
                if (chain, way, step - 1) not in ring:
                    continue
                ring[chain, way, step - 1].wait_recv()
                origin = (y + (8 - step if way == 0 else step)) % 8
                piece = shard(zl if chain == 0 else 1 - zl, origin, core)
                if step < 3 or (step == 3 and chain == way):
                    to_ring(chain, way, step, piece, piece)
                to_core(piece, piece)

    @pl.when(jnp.logical_not(stays))
    def _():
        row_copy.wait_recv()

    @pl.when(stays)
    def _():
        row_keep.wait()

    def columns_of(k):
        return pl.ds(pl.multiple_of(k * B, B), B)

    def band(at, size):
        return own_rows.at[pl.ds(pl.multiple_of(at, 16), size)]

    slices = [
        send(
            row_in.at[:, columns_of((x + i) % 4)],
            band(share * ROWS, ROWS),
            slice_send.at[i - 1],
            slice_recv.at[i - 1],
            x_device(i),
        )
        for i in (1, 3, 2)
    ]
    slice_keep = pltpu.make_async_copy(
        row_in.at[:, columns_of(x)], band(share * ROWS, ROWS), local_sem.at[3]
    )
    slice_keep.start()
    keep.wait()
    big_copy.wait()
    for copy in core_copies:
        copy.wait_recv()

    for j in range(6):
        rows = pl.ds(j * B, B)
        listed = jnp.max(jnp.where(lists[...] == r * 6 + j, 1.0, 0.0), axis=1, keepdims=True)
        for k in range(NK):
            columns = pl.ds(k * B, B)
            value = gathered[rows, columns].astype(F32) * -listed[k : k + 1, :]
            masked[rows, columns] = value.astype(BF16)

    def multiply(k):
        columns = columns_of(k)

        @pl.loop(0, 2)
        def _(half):
            rows = pl.ds(pl.multiple_of(half * 384, 128), 384)
            product = jnp.dot(inverse[rows, :], masked[:, columns], preferred_element_type=F32)
            part[k, half] = product.reshape(CHUNKS, CHUNK, B)

    def hop(source, target, sends, recvs, chunk, n, device):
        at = chunk * 6 + n
        return send(source, target.at[chunk, n], sends.at[at], recvs.at[at], device)

    far, ahead, behind = (x + 2) % 4, (x + 1) % 4, (x + 3) % 4
    hops = {}

    def x_mid(h):
        hops["x", h, 0] = hop(part.at[far, 0, h], x_in, x_send, x_recv, h, 0, x_device(1))
        hops["x", h, 1] = hop(part.at[far, 1, h], x_in, x_send, x_recv, h, 1, x_device(-1))

    def x_raw_up(h):
        hops["x", h, 2] = hop(part.at[ahead, 1, h], x_in, x_send, x_recv, h, 2, x_device(1))

    def x_raw_down(h):
        hops["x", h, 4] = hop(part.at[behind, 0, h], x_in, x_send, x_recv, h, 4, x_device(-1))

    def x_sum(h):
        hops["x", h, 0].wait_recv()
        part[ahead, 0, h] = part[ahead, 0, h] + x_in[h, 0]
        hops["x", h, 3] = hop(part.at[ahead, 0, h], x_in, x_send, x_recv, h, 3, x_device(1))
        hops["x", h, 1].wait_recv()
        part[behind, 1, h] = part[behind, 1, h] + x_in[h, 1]
        hops["x", h, 5] = hop(part.at[behind, 1, h], x_in, x_send, x_recv, h, 5, x_device(-1))

    z_far, z_ahead, z_behind = (zh + 2) % 4, (zh + 1) % 4, (zh + 3) % 4

    def z_start(h):
        for n in (2, 3, 4, 5):
            hops["x", h, n].wait_recv()
        for way in range(2):
            rows = pl.ds(way * (CHUNK // 2), CHUNK // 2)
            low = part[x, 0, h, rows, :] + x_in[h, 3, rows, :] + x_in[h, 4, rows, :]
            high = part[x, 1, h, rows, :] + x_in[h, 5, rows, :] + x_in[h, 2, rows, :]
            for q in range(4):
                lanes = slice(64 * q, 64 * q + 64)
                z_part[q, h, way] = jnp.concatenate([low[:, lanes], high[:, lanes]], axis=1)
        up, down = z_device(1), z_device(-1)
        hops["z", h, 0] = hop(z_part.at[z_far, h, 0], z_in, z_send, z_recv, h, 0, up)
        hops["z", h, 1] = hop(z_part.at[z_far, h, 1], z_in, z_send, z_recv, h, 1, down)
        hops["z", h, 2] = hop(z_part.at[z_ahead, h, 1], z_in, z_send, z_recv, h, 2, up)
        hops["z", h, 4] = hop(z_part.at[z_behind, h, 0], z_in, z_send, z_recv, h, 4, down)

    def z_sum(h):
        hops["z", h, 0].wait_recv()
        z_part[z_ahead, h, 0] = z_part[z_ahead, h, 0] + z_in[h, 0]
        hops["z", h, 3] = hop(z_part.at[z_ahead, h, 0], z_in, z_send, z_recv, h, 3, z_device(1))
        hops["z", h, 1].wait_recv()
        z_part[z_behind, h, 1] = z_part[z_behind, h, 1] + z_in[h, 1]
        hops["z", h, 5] = hop(z_part.at[z_behind, h, 1], z_in, z_send, z_recv, h, 5, z_device(-1))

    def band_copy(n, at, size, device):
        here = band(at, size)
        return send(here, here, band_send.at[n], band_recv.at[n], device)

    multiply(far)
    x_mid(0)
    multiply(ahead)
    x_raw_up(0)
    multiply(behind)
    x_raw_down(0)
    if CHUNKS > 1:
        x_mid(1)
    slice_keep.wait()
    for copy in slices:
        copy.wait_recv()
    band_up = band_copy(0, zh * 192, 192, z_device(1))
    band_down = band_copy(1, zh * 192, 192, z_device(-1))
    multiply(x)
    far_up = far_down = None
    for h in range(CHUNKS):
        x_sum(h)
        if h + 1 < CHUNKS:
            x_raw_up(h + 1)
            x_raw_down(h + 1)
        if h + 2 < CHUNKS:
            x_mid(h + 2)
        if h == 0:
            band_up.wait_recv()
            far_up = band_copy(2, z_behind * 192, 96, z_device(1))
            band_down.wait_recv()
            far_down = band_copy(3, z_ahead * 192 + 96, 96, z_device(-1))
        if h >= 2:
            z_sum(h - 2)
        if h >= 1:
            z_start(h - 1)
    if CHUNKS > 1:
        z_sum(CHUNKS - 2)
    z_start(CHUNKS - 1)
    z_sum(CHUNKS - 1)
    far_up.wait_recv()
    far_down.wait_recv()

    half_rows = CHUNK // 2
    lane = lax.broadcasted_iota(jnp.int32, (half_rows, 128), 1)
    row = lax.broadcasted_iota(jnp.int32, (half_rows, 128), 0) + jnp.where(lane < 64, 0, 384)
    kept = [
        jnp.max(jnp.where(lists[...] == c * 3 + i, 1.0, 0.0), axis=1, keepdims=True)
        for i in range(3)
    ]
    level = lax.broadcasted_iota(jnp.int32, (NK, 1), 0) == x
    kept = [jnp.sum(jnp.where(level, k, 0.0), axis=0, keepdims=True) for k in kept]
    left_sum = jnp.zeros((B, 128), F32)
    right_sum = jnp.zeros((B, 128), F32)
    over_rows = (((0,), (0,)), ((), ()))
    for h in range(CHUNKS):
        for n in (2, 3, 4, 5):
            hops["z", h, n].wait_recv()
        for way in range(2):
            start = h * CHUNK + way * half_rows
            at = row + start
            keep_row = jnp.where(at < B, kept[0], jnp.where(at < 2 * B, kept[1], kept[2]))
            first, second = (3, 4) if way == 0 else (5, 2)
            total = (z_part[zh, h, way] + z_in[h, first] + z_in[h, second]) * keep_row
            off_out[pl.ds(start, half_rows), :] = total[:, :64].astype(BF16)
            off_out[pl.ds(384 + start, half_rows), :] = total[:, 64:].astype(BF16)
            big = total.astype(BF16)
            small = (total - big.astype(F32)).astype(BF16)
            left = own_rows[pl.ds(start, half_rows), :]
            right = own_rows[pl.ds(384 + start, half_rows), :]
            for piece in (big, small):
                left_sum = left_sum + lax.dot_general(
                    left, piece, over_rows, preferred_element_type=F32
                )
                right_sum = right_sum + lax.dot_general(
                    right, piece, over_rows, preferred_element_type=F32
                )
    lane = lax.broadcasted_iota(jnp.int32, (B, 128), 1)
    term = jnp.where(lane < 64, left_sum, right_sum).reshape(2, 8, 2, 8, 128)

    for q in range(2):
        core_part[q] = term[:, :, q]
    copy = send(
        core_part.at[1 - core], core_in, sum_sem.at[0], sum_sem.at[1], col_device(zl, y, 1 - core)
    )
    copy.wait_recv()
    pair_part[...] = core_part[core] + core_in[...]
    copy = send(
        pair_part.at[1 - zl], pair_in, sum_sem.at[2], sum_sem.at[3], col_device(1 - zl, y, core)
    )
    copy.wait_recv()
    y_part[...] = pair_part[zl] + pair_in[...]
    y_copies = [
        send(
            y_part.at[(y + i) % 8],
            y_in.at[i - 1],
            y_send.at[i - 1],
            y_recv.at[i - 1],
            col_device(zl, y + i, core),
        )
        for i in range(1, 8)
    ]
    pivot_copy.wait()
    total = y_part[y]
    for i, copy in enumerate(y_copies):
        copy.wait_recv()
        total = total + y_in[i]
    diag_out[...] = pivot[...] - (total[:, :64] + total[:, 64:])

    for copy in sent:
        copy.wait_send()

    @pl.when(jnp.logical_not(stays))
    def _():
        row_copy.wait_send()


def body(ancestor_inverse, lower_panel, pivot_inverse, struct_list):
    vmem = pl.BlockSpec(memory_space=pltpu.VMEM)
    hbm = pl.BlockSpec(memory_space=pltpu.HBM)
    dma = pltpu.SemaphoreType.DMA
    hop_sems = [dma((6 * CHUNKS,))] * 4
    return pl.pallas_call(
        kernel,
        out_shape=(
            jax.ShapeDtypeStruct((768, 64), BF16),
            jax.ShapeDtypeStruct((8, 64), F32),
        ),
        in_specs=[vmem, hbm, hbm, hbm],
        out_specs=(vmem, vmem),
        scratch_shapes=[
            pltpu.VMEM((768, 1536), BF16),
            pltpu.VMEM((8, 64), F32),
            pltpu.VMEM((1536, 1024), BF16),
            pltpu.VMEM((1536, 1024), BF16),
            pltpu.VMEM((48, 1024), BF16),
            pltpu.VMEM((768, B), BF16),
            pltpu.VMEM((4, 2, CHUNKS, CHUNK, B), F32),
            pltpu.VMEM((CHUNKS, 6, CHUNK, B), F32),
            pltpu.VMEM((4, CHUNKS, 2, CHUNK // 2, 128), F32),
            pltpu.VMEM((CHUNKS, 6, CHUNK // 2, 128), F32),
            pltpu.VMEM((2, 2, 8, 8, 128), F32),
            pltpu.VMEM((2, 8, 8, 128), F32),
            pltpu.VMEM((2, 8, 8, 128), F32),
            pltpu.VMEM((8, 8, 128), F32),
            pltpu.VMEM((8, 8, 128), F32),
            pltpu.VMEM((7, 8, 128), F32),
            dma((4,)),
            dma((2,)),
            dma((16,)),
            dma((16,)),
            dma((16,)),
            dma((16,)),
            dma((3,)),
            dma((3,)),
            dma((3,)),
            dma((4,)),
            dma((4,)),
            *hop_sems,
            dma((4,)),
            dma((7,)),
            dma((7,)),
        ],
        compiler_params=pltpu.CompilerParams(
            collective_id=0, has_side_effects=True
        ),
    )(struct_list, ancestor_inverse, lower_panel, pivot_inverse)


def solution(mesh):
    placed = (P("pcol", "prow"), P(("prow", "pcol"), None), P("pcol", "prow"), P())
    return jax.shard_map(
        body,
        mesh=mesh,
        in_specs=placed,
        out_specs=(P("pcol", "prow"), P("pcol", "prow")),
        check_vma=False,
    )
```

time: 581 us -> 101 us (0.17)
  waiting for transfers between devices: 539 us -> 0 us
  Pallas kernels: 0 us -> 97.2 us
  between operations: 14.6 us -> 0.64 us
  other arithmetic: 9.68 us -> 0 us
  matrix products: 8.3 us -> 0 us
    unnamed x5 -> x0, waiting for transfers between devices: 198 us -> none
    psum x1 -> x0, waiting for transfers between devices: 160 us -> none  [from_root(): return lax.psum(jnp.where(mine, value, jnp.zeros_like(value)), axis)]
    reduce_scatter x1 -> x0, waiting for transfers between devices: 109 us -> none  [body(): lax.psum_scatter(partial_value, 'prow', scatter_dimension=1, tiled=True)]
    pallas_call x0 -> x1, Pallas kernels: none -> 97.2 us  [body(): pl.pallas_call(kernel, out_shape=(jax.ShapeDtypeStruct((768, 64), BF16),...]
    all_gather x1 -> x0, waiting for transfers between devices: 72.4 us -> none  [body(): gathered = lax.all_gather(lower_panel, 'pcol', axis=0, tiled=True)]
    dot_general x2 -> x0, matrix products: 8.3 us -> none  [the longest x1 6.25 us: body(): jnp.dot(ancestor_inverse, masked, preferred_element_type=jnp.float32)]
  transfers between devices with their start and end apart: 4 -> 0, of which waited for: 4 -> 0; matrix products, arithmetic and copies ran while one was open for 2% -> 0% of each run, Pallas kernels for 0% -> 0%
where the time goes in v2:
time: 101 us
  Pallas kernels  97.2 us (96%)
  local copies, waits for them, and re-layouts  2.95 us (3%)
    pallas_call x1, Pallas kernels, body(): pl.pallas_call(kernel, out_shape=(jax.ShapeDtypeStruct((768, 64), BF16),...  97.2 us

profile of v2, /device:TPU:1, one launch (start us, length us, event | category | flops | bytes accessed | tf_op | source)
XLA Modules:
  0.0 100.8 jit_solution(2653066715270411520)
XLA Ops:
  0.6 97.2 %shard_map.59 = (bf16[768,64]{1,0:T(8,128)(2,1)}, f32[8,64]{1,0:T(8,128)}) custom-call(s32[4,48]{1,0:T(4,128)} %lists.1, bf16[768,1536]{1,0:T(8,128)(2,1)} %inverse_hbm.1, bf16[48,1024]{1,0:T(8,128)(2,1)} %lower.1, f32[8,64]{1,0:T(8,128)} %pivot_hbm.1), custom_call_target="tpu_custom_call" | custom-call | tf_op jit(solution)/shard_map/pallas_call | solution.py:387
  97.9 1.7 %copy.6 = bf16[768,64]{0,1:T(8,128)(2,1)} copy(bf16[768,64]{1,0:T(8,128)(2,1)} %get-tuple-element.2) | data formatting | bytes 196608 | tf_op jit(solution)/shard_map/pallas_call | solution.py:387
  99.5 1.3 %copy.8 = f32[8,64]{1,0:T(8,128)} copy(f32[8,64]{1,0:T(8,128)} %get-tuple-element.7) | data formatting | bytes 4096

commit v3 on v2

--- a/solution.py
+++ b/solution.py
@@ -12,7 +12,7 @@
 BF16 = jnp.bfloat16
 ROWS = 48
 SHARES = 16
-CHUNKS = 2
+CHUNKS = 3
 CHUNK = 384 // CHUNKS
 
 
@@ -25,14 +25,15 @@
 def kernel(
     lists,
     inverse_hbm,
-    lower,
+    lower_hbm,
     pivot_hbm,
     off_out,
     diag_out,
     inverse,
     pivot,
+    raw,
+    lower,
     gathered,
-    masked,
     row_in,
     own_rows,
     part,
@@ -41,8 +42,6 @@
     z_in,
     core_part,
     core_in,
-    pair_part,
-    pair_in,
     y_part,
     y_in,
     local_sem,
@@ -86,9 +85,12 @@
     pivot_copy = pltpu.make_async_copy(pivot_hbm, pivot, local_sem.at[2])
     pivot_copy.start()
 
+    raw_copy = pltpu.make_async_copy(lower_hbm, raw, local_sem.at[4])
+    raw_copy.start()
+
     barrier = pltpu.get_barrier_semaphore()
     friends = [col_device(zl, y + i, core) for i in range(1, 8)]
-    friends += [col_device(zl, y, 1 - core), col_device(1 - zl, y, core)]
+    friends += [col_device(1 - zl, y + i, core) for i in range(8)] + [col_device(zl, y, 1 - core)]
     friends += [x_device(1), x_device(2), x_device(3), z_device(1), z_device(-1)]
     for device in friends:
         pl.semaphore_signal(barrier, inc=1, device_id=device, device_id_type=MESH)
@@ -96,6 +98,20 @@
     @pl.when(jnp.logical_not(stays))
     def _():
         pl.semaphore_signal(barrier, inc=1, device_id=source, device_id_type=MESH)
+
+    def listed(ancestor):
+        found = jnp.where(lists[...] == ancestor, 1.0, 0.0)
+        return jnp.max(found, axis=1, keepdims=True)
+
+    raw_copy.wait()
+    begin = (r * 32 + c) * ROWS
+    first = begin // B
+    in_first = lax.broadcasted_iota(jnp.int32, (ROWS, B), 0) + begin < (first + 1) * B
+    of_first, of_next = listed(first), listed(first + 1)
+    for k in range(NK):
+        columns = pl.ds(k * B, B)
+        member = jnp.where(in_first, of_first[k : k + 1, :], of_next[k : k + 1, :])
+        lower[:, columns] = (raw[:, columns].astype(F32) * member).astype(BF16)
 
     pl.semaphore_wait(barrier, len(friends) + 1 - stays.astype(jnp.int32))
 
@@ -137,19 +153,19 @@
     )
     row_keep = pltpu.make_async_copy(lower, row_in, row_sem.at[2])
 
-    @pl.when(jnp.logical_not(stays))
-    def _():
-        row_copy.start()
-
-    @pl.when(stays)
-    def _():
-        row_keep.start()
-
     pair.wait_recv()
     theirs = shard(1 - zl, y, core)
     to_ring(1, 0, 0, theirs, theirs)
     to_ring(1, 1, 0, theirs, theirs)
     to_core(theirs, theirs)
+    pair_copies = [pair]
+
+    def to_pair(piece):
+        n = len(pair_copies)
+        pair_copies.append(
+            send(piece, piece, pair_sem.at[2 * n], pair_sem.at[2 * n + 1], col_device(1 - zl, y, core))
+        )
+
     for step in range(1, 5):
         for chain in range(2):
             for way in range(2):
@@ -158,17 +174,24 @@
                 ring[chain, way, step - 1].wait_recv()
                 origin = (y + (8 - step if way == 0 else step)) % 8
                 piece = shard(zl if chain == 0 else 1 - zl, origin, core)
-                if step < 3 or (step == 3 and chain == way):
+                if step < (3 if chain == 0 else 2) or (step == 3 and (chain, way) == (0, 0)):
                     to_ring(chain, way, step, piece, piece)
+                if chain == 0 and step >= 3:
+                    to_pair(piece)
                 to_core(piece, piece)
 
     @pl.when(jnp.logical_not(stays))
     def _():
-        row_copy.wait_recv()
+        row_copy.start()
 
     @pl.when(stays)
     def _():
-        row_keep.wait()
+        row_keep.start()
+
+    for copy, origin in zip(pair_copies[1:], (y + 5, y + 3, y + 4)):
+        copy.wait_recv()
+        piece = shard(1 - zl, origin % 8, core)
+        to_core(piece, piece)
 
     def columns_of(k):
         return pl.ds(pl.multiple_of(k * B, B), B)
@@ -176,40 +199,18 @@
     def band(at, size):
         return own_rows.at[pl.ds(pl.multiple_of(at, 16), size)]
 
-    slices = [
-        send(
-            row_in.at[:, columns_of((x + i) % 4)],
-            band(share * ROWS, ROWS),
-            slice_send.at[i - 1],
-            slice_recv.at[i - 1],
-            x_device(i),
-        )
-        for i in (1, 3, 2)
-    ]
-    slice_keep = pltpu.make_async_copy(
-        row_in.at[:, columns_of(x)], band(share * ROWS, ROWS), local_sem.at[3]
-    )
-    slice_keep.start()
     keep.wait()
     big_copy.wait()
     for copy in core_copies:
         copy.wait_recv()
 
-    for j in range(6):
-        rows = pl.ds(j * B, B)
-        listed = jnp.max(jnp.where(lists[...] == r * 6 + j, 1.0, 0.0), axis=1, keepdims=True)
-        for k in range(NK):
-            columns = pl.ds(k * B, B)
-            value = gathered[rows, columns].astype(F32) * -listed[k : k + 1, :]
-            masked[rows, columns] = value.astype(BF16)
-
     def multiply(k):
         columns = columns_of(k)
 
         @pl.loop(0, 2)
         def _(half):
             rows = pl.ds(pl.multiple_of(half * 384, 128), 384)
-            product = jnp.dot(inverse[rows, :], masked[:, columns], preferred_element_type=F32)
+            product = jnp.dot(inverse[rows, :], gathered[:, columns], preferred_element_type=F32)
             part[k, half] = product.reshape(CHUNKS, CHUNK, B)
 
     def hop(source, target, sends, recvs, chunk, n, device):
@@ -275,13 +276,30 @@
     x_raw_down(0)
     if CHUNKS > 1:
         x_mid(1)
-    slice_keep.wait()
-    for copy in slices:
-        copy.wait_recv()
-    band_up = band_copy(0, zh * 192, 192, z_device(1))
-    band_down = band_copy(1, zh * 192, 192, z_device(-1))
     multiply(x)
-    far_up = far_down = None
+
+    @pl.when(jnp.logical_not(stays))
+    def _():
+        row_copy.wait_recv()
+
+    @pl.when(stays)
+    def _():
+        row_keep.wait()
+
+    slices = [
+        send(
+            row_in.at[:, columns_of((x + i) % 4)],
+            band(share * ROWS, ROWS),
+            slice_send.at[i - 1],
+            slice_recv.at[i - 1],
+            x_device(i),
+        )
+        for i in (1, 3, 2)
+    ]
+    slice_keep = pltpu.make_async_copy(
+        row_in.at[:, columns_of(x)], band(share * ROWS, ROWS), local_sem.at[3]
+    )
+    slice_keep.start()
     for h in range(CHUNKS):
         x_sum(h)
         if h + 1 < CHUNKS:
@@ -290,6 +308,12 @@
         if h + 2 < CHUNKS:
             x_mid(h + 2)
         if h == 0:
+            slice_keep.wait()
+            for copy in slices:
+                copy.wait_recv()
+            band_up = band_copy(0, zh * 192, 192, z_device(1))
+            band_down = band_copy(1, zh * 192, 192, z_device(-1))
+        if h == 1:
             band_up.wait_recv()
             far_up = band_copy(2, z_behind * 192, 96, z_device(1))
             band_down.wait_recv()
@@ -308,10 +332,7 @@
     half_rows = CHUNK // 2
     lane = lax.broadcasted_iota(jnp.int32, (half_rows, 128), 1)
     row = lax.broadcasted_iota(jnp.int32, (half_rows, 128), 0) + jnp.where(lane < 64, 0, 384)
-    kept = [
-        jnp.max(jnp.where(lists[...] == c * 3 + i, 1.0, 0.0), axis=1, keepdims=True)
-        for i in range(3)
-    ]
+    kept = [-listed(c * 3 + i) for i in range(3)]
     level = lax.broadcasted_iota(jnp.int32, (NK, 1), 0) == x
     kept = [jnp.sum(jnp.where(level, k, 0.0), axis=0, keepdims=True) for k in kept]
     left_sum = jnp.zeros((B, 128), F32)
@@ -348,27 +369,24 @@
         core_part.at[1 - core], core_in, sum_sem.at[0], sum_sem.at[1], col_device(zl, y, 1 - core)
     )
     copy.wait_recv()
-    pair_part[...] = core_part[core] + core_in[...]
-    copy = send(
-        pair_part.at[1 - zl], pair_in, sum_sem.at[2], sum_sem.at[3], col_device(1 - zl, y, core)
-    )
-    copy.wait_recv()
-    y_part[...] = pair_part[zl] + pair_in[...]
-    y_copies = [
-        send(
-            y_part.at[(y + i) % 8],
-            y_in.at[i - 1],
-            y_send.at[i - 1],
-            y_recv.at[i - 1],
-            col_device(zl, y + i, core),
+    y_part[...] = core_part[core] + core_in[...]
+    y_copies = []
+    for n in range(1, 16):
+        z_to, y_to = (zl + n // 8) % 2, (y + n) % 8
+        y_copies.append(
+            send(
+                y_part.at[z_to, y_to],
+                y_in.at[n - 1],
+                y_send.at[n - 1],
+                y_recv.at[n - 1],
+                col_device(z_to, y_to, core),
+            )
         )
-        for i in range(1, 8)
-    ]
     pivot_copy.wait()
-    total = y_part[y]
-    for i, copy in enumerate(y_copies):
+    total = y_part[zl, y]
+    for n, copy in enumerate(y_copies):
         copy.wait_recv()
-        total = total + y_in[i]
+        total = total + y_in[n]
     diag_out[...] = pivot[...] - (total[:, :64] + total[:, 64:])
 
     for copy in sent:
@@ -395,9 +413,10 @@
         scratch_shapes=[
             pltpu.VMEM((768, 1536), BF16),
             pltpu.VMEM((8, 64), F32),
+            pltpu.VMEM((ROWS, 1024), BF16),
+            pltpu.VMEM((ROWS, 1024), BF16),
             pltpu.VMEM((1536, 1024), BF16),
-            pltpu.VMEM((1536, 1024), BF16),
-            pltpu.VMEM((48, 1024), BF16),
+            pltpu.VMEM((ROWS, 1024), BF16),
             pltpu.VMEM((768, B), BF16),
             pltpu.VMEM((4, 2, CHUNKS, CHUNK, B), F32),
             pltpu.VMEM((CHUNKS, 6, CHUNK, B), F32),
@@ -406,11 +425,9 @@
             pltpu.VMEM((2, 2, 8, 8, 128), F32),
             pltpu.VMEM((2, 8, 8, 128), F32),
             pltpu.VMEM((2, 8, 8, 128), F32),
-            pltpu.VMEM((8, 8, 128), F32),
-            pltpu.VMEM((8, 8, 128), F32),
-            pltpu.VMEM((7, 8, 128), F32),
-            dma((4,)),
-            dma((2,)),
+            pltpu.VMEM((15, 8, 128), F32),
+            dma((5,)),
+            dma((8,)),
             dma((16,)),
             dma((16,)),
             dma((16,)),
@@ -421,9 +438,9 @@
             dma((4,)),
             dma((4,)),
             *hop_sems,
-            dma((4,)),
-            dma((7,)),
-            dma((7,)),
+            dma((2,)),
+            dma((15,)),
+            dma((15,)),
         ],
         compiler_params=pltpu.CompilerParams(
             collective_id=0, has_side_effects=True

time: 101 us -> 104 us (1.030)
  Pallas kernels: 97.2 us -> 100 us
    pallas_call x1, Pallas kernels: 97.2 us -> 100 us  [body(): pl.pallas_call(kernel, out_shape=(jax.ShapeDtypeStruct((768, 64), BF16),...]
where the time goes in v3:
time: 104 us
  Pallas kernels  100 us (96%)
  local copies, waits for them, and re-layouts  2.95 us (3%)
    pallas_call x1, Pallas kernels, body(): pl.pallas_call(kernel, out_shape=(jax.ShapeDtypeStruct((768, 64), BF16),...  100 us

profile of v3, /device:TPU:1, one launch (start us, length us, event | category | flops | bytes accessed | tf_op | source)
XLA Modules:
  0.0 104.0 jit_solution(15677418903996202145)
XLA Ops:
  0.6 100.4 %shard_map.59 = (bf16[768,64]{1,0:T(8,128)(2,1)}, f32[8,64]{1,0:T(8,128)}) custom-call(s32[4,48]{1,0:T(4,128)} %lists.1, bf16[768,1536]{1,0:T(8,128)(2,1)} %inverse_hbm.1, bf16[48,1024]{1,0:T(8,128)(2,1)} %lower_hbm.1, f32[8,64]{1,0:T(8,128)} %pivot_hbm.1), custom_call_target="tpu_custom_call" | custom-call | tf_op jit(solution)/shard_map/pallas_call | solution.py:405
  101.1 1.7 %copy.6 = bf16[768,64]{0,1:T(8,128)(2,1)} copy(bf16[768,64]{1,0:T(8,128)(2,1)} %get-tuple-element.2) | data formatting | bytes 196608 | tf_op jit(solution)/shard_map/pallas_call | solution.py:405
  102.8 1.3 %copy.8 = f32[8,64]{1,0:T(8,128)} copy(f32[8,64]{1,0:T(8,128)} %get-tuple-element.7) | data formatting | bytes 4096

commit v4 on v3

--- a/solution.py
+++ b/solution.py
@@ -12,7 +12,7 @@
 BF16 = jnp.bfloat16
 ROWS = 48
 SHARES = 16
-CHUNKS = 3
+CHUNKS = 2
 CHUNK = 384 // CHUNKS
 
 
@@ -158,13 +158,13 @@
     to_ring(1, 0, 0, theirs, theirs)
     to_ring(1, 1, 0, theirs, theirs)
     to_core(theirs, theirs)
-    pair_copies = [pair]
-
-    def to_pair(piece):
-        n = len(pair_copies)
-        pair_copies.append(
-            send(piece, piece, pair_sem.at[2 * n], pair_sem.at[2 * n + 1], col_device(1 - zl, y, core))
-        )
+    @pl.when(jnp.logical_not(stays))
+    def _():
+        row_copy.start()
+
+    @pl.when(stays)
+    def _():
+        row_keep.start()
 
     for step in range(1, 5):
         for chain in range(2):
@@ -174,24 +174,9 @@
                 ring[chain, way, step - 1].wait_recv()
                 origin = (y + (8 - step if way == 0 else step)) % 8
                 piece = shard(zl if chain == 0 else 1 - zl, origin, core)
-                if step < (3 if chain == 0 else 2) or (step == 3 and (chain, way) == (0, 0)):
+                if step < 3 or (step == 3 and chain == way):
                     to_ring(chain, way, step, piece, piece)
-                if chain == 0 and step >= 3:
-                    to_pair(piece)
                 to_core(piece, piece)
-
-    @pl.when(jnp.logical_not(stays))
-    def _():
-        row_copy.start()
-
-    @pl.when(stays)
-    def _():
-        row_keep.start()
-
-    for copy, origin in zip(pair_copies[1:], (y + 5, y + 3, y + 4)):
-        copy.wait_recv()
-        piece = shard(1 - zl, origin % 8, core)
-        to_core(piece, piece)
 
     def columns_of(k):
         return pl.ds(pl.multiple_of(k * B, B), B)
@@ -427,7 +412,7 @@
             pltpu.VMEM((2, 8, 8, 128), F32),
             pltpu.VMEM((15, 8, 128), F32),
             dma((5,)),
-            dma((8,)),
+            dma((2,)),
             dma((16,)),
             dma((16,)),
             dma((16,)),

time: 104 us -> 105 us (level); the launches traced: 104 us -> 104 us
  no operation moved by 1% of the time
where the time goes in v4:
time: 105 us; the launch traced here: 104 us
  Pallas kernels  100 us (95%)
  local copies, waits for them, and re-layouts  2.95 us (3%)
    pallas_call x1, Pallas kernels, body(): pl.pallas_call(kernel, out_shape=(jax.ShapeDtypeStruct((768, 64), BF16),...  100 us

profile of v4, /device:TPU:1, one launch (start us, length us, event | category | flops | bytes accessed | tf_op | source)
XLA Modules:
  0.0 104.0 jit_solution(8365421587198884075)
XLA Ops:
  0.6 100.4 %shard_map.59 = (bf16[768,64]{1,0:T(8,128)(2,1)}, f32[8,64]{1,0:T(8,128)}) custom-call(s32[4,48]{1,0:T(4,128)} %lists.1, bf16[768,1536]{1,0:T(8,128)(2,1)} %inverse_hbm.1, bf16[48,1024]{1,0:T(8,128)(2,1)} %lower_hbm.1, f32[8,64]{1,0:T(8,128)} %pivot_hbm.1), custom_call_target="tpu_custom_call" | custom-call | tf_op jit(solution)/shard_map/pallas_call | solution.py:390
  101.0 1.7 %copy.6 = bf16[768,64]{0,1:T(8,128)(2,1)} copy(bf16[768,64]{1,0:T(8,128)(2,1)} %get-tuple-element.2) | data formatting | bytes 196608 | tf_op jit(solution)/shard_map/pallas_call | solution.py:390
  102.7 1.3 %copy.8 = f32[8,64]{1,0:T(8,128)} copy(f32[8,64]{1,0:T(8,128)} %get-tuple-element.7) | data formatting | bytes 4096

commit v5 on v4

--- a/solution.py
+++ b/solution.py
@@ -158,14 +158,6 @@
     to_ring(1, 0, 0, theirs, theirs)
     to_ring(1, 1, 0, theirs, theirs)
     to_core(theirs, theirs)
-    @pl.when(jnp.logical_not(stays))
-    def _():
-        row_copy.start()
-
-    @pl.when(stays)
-    def _():
-        row_keep.start()
-
     for step in range(1, 5):
         for chain in range(2):
             for way in range(2):
@@ -177,6 +169,14 @@
                 if step < 3 or (step == 3 and chain == way):
                     to_ring(chain, way, step, piece, piece)
                 to_core(piece, piece)
+
+    @pl.when(jnp.logical_not(stays))
+    def _():
+        row_copy.start()
+
+    @pl.when(stays)
+    def _():
+        row_keep.start()
 
     def columns_of(k):
         return pl.ds(pl.multiple_of(k * B, B), B)
@@ -263,6 +263,12 @@
         x_mid(1)
     multiply(x)
 
+    x_sum(0)
+    x_raw_up(1)
+    x_raw_down(1)
+    x_sum(1)
+    z_start(0)
+
     @pl.when(jnp.logical_not(stays))
     def _():
         row_copy.wait_recv()
@@ -285,32 +291,18 @@
         row_in.at[:, columns_of(x)], band(share * ROWS, ROWS), local_sem.at[3]
     )
     slice_keep.start()
-    for h in range(CHUNKS):
-        x_sum(h)
-        if h + 1 < CHUNKS:
-            x_raw_up(h + 1)
-            x_raw_down(h + 1)
-        if h + 2 < CHUNKS:
-            x_mid(h + 2)
-        if h == 0:
-            slice_keep.wait()
-            for copy in slices:
-                copy.wait_recv()
-            band_up = band_copy(0, zh * 192, 192, z_device(1))
-            band_down = band_copy(1, zh * 192, 192, z_device(-1))
-        if h == 1:
-            band_up.wait_recv()
-            far_up = band_copy(2, z_behind * 192, 96, z_device(1))
-            band_down.wait_recv()
-            far_down = band_copy(3, z_ahead * 192 + 96, 96, z_device(-1))
-        if h >= 2:
-            z_sum(h - 2)
-        if h >= 1:
-            z_start(h - 1)
-    if CHUNKS > 1:
-        z_sum(CHUNKS - 2)
-    z_start(CHUNKS - 1)
-    z_sum(CHUNKS - 1)
+    z_sum(0)
+    slice_keep.wait()
+    for copy in slices:
+        copy.wait_recv()
+    band_up = band_copy(0, zh * 192, 192, z_device(1))
+    band_down = band_copy(1, zh * 192, 192, z_device(-1))
+    z_start(1)
+    z_sum(1)
+    band_up.wait_recv()
+    far_up = band_copy(2, z_behind * 192, 96, z_device(1))
+    band_down.wait_recv()
+    far_down = band_copy(3, z_ahead * 192 + 96, 96, z_device(-1))
     far_up.wait_recv()
     far_down.wait_recv()
 

time: 105 us -> 101 us (0.962)
  Pallas kernels: 100 us -> 97.3 us
    pallas_call x1, Pallas kernels: 100 us -> 97.3 us  [body(): pl.pallas_call(kernel, out_shape=(jax.ShapeDtypeStruct((768, 64), BF16),...]
where the time goes in v5:
time: 101 us
  Pallas kernels  97.3 us (96%)
  local copies, waits for them, and re-layouts  2.95 us (3%)
    pallas_call x1, Pallas kernels, body(): pl.pallas_call(kernel, out_shape=(jax.ShapeDtypeStruct((768, 64), BF16),...  97.3 us

profile of v5, /device:TPU:1, one launch (start us, length us, event | category | flops | bytes accessed | tf_op | source)
XLA Modules:
  0.0 100.9 jit_solution(14154203035119310484)
XLA Ops:
  0.6 97.3 %shard_map.59 = (bf16[768,64]{1,0:T(8,128)(2,1)}, f32[8,64]{1,0:T(8,128)}) custom-call(s32[4,48]{1,0:T(4,128)} %lists.1, bf16[768,1536]{1,0:T(8,128)(2,1)} %inverse_hbm.1, bf16[48,1024]{1,0:T(8,128)(2,1)} %lower_hbm.1, f32[8,64]{1,0:T(8,128)} %pivot_hbm.1), custom_call_target="tpu_custom_call" | custom-call | tf_op jit(solution)/shard_map/pallas_call | solution.py:382
  98.0 1.7 %copy.6 = bf16[768,64]{0,1:T(8,128)(2,1)} copy(bf16[768,64]{1,0:T(8,128)(2,1)} %get-tuple-element.2) | data formatting | bytes 196608 | tf_op jit(solution)/shard_map/pallas_call | solution.py:382
  99.7 1.3 %copy.8 = f32[8,64]{1,0:T(8,128)} copy(f32[8,64]{1,0:T(8,128)} %get-tuple-element.7) | data formatting | bytes 4096

commit v6 on v4

--- a/solution.py
+++ b/solution.py
@@ -153,19 +153,19 @@
     )
     row_keep = pltpu.make_async_copy(lower, row_in, row_sem.at[2])
 
+    @pl.when(jnp.logical_not(stays))
+    def _():
+        row_copy.start()
+
+    @pl.when(stays)
+    def _():
+        row_keep.start()
+
     pair.wait_recv()
     theirs = shard(1 - zl, y, core)
     to_ring(1, 0, 0, theirs, theirs)
     to_ring(1, 1, 0, theirs, theirs)
     to_core(theirs, theirs)
-    @pl.when(jnp.logical_not(stays))
-    def _():
-        row_copy.start()
-
-    @pl.when(stays)
-    def _():
-        row_keep.start()
-
     for step in range(1, 5):
         for chain in range(2):
             for way in range(2):
@@ -184,6 +184,28 @@
     def band(at, size):
         return own_rows.at[pl.ds(pl.multiple_of(at, 16), size)]
 
+    @pl.when(jnp.logical_not(stays))
+    def _():
+        row_copy.wait_recv()
+
+    @pl.when(stays)
+    def _():
+        row_keep.wait()
+
+    slices = [
+        send(
+            row_in.at[:, columns_of((x + i) % 4)],
+            band(share * ROWS, ROWS),
+            slice_send.at[i - 1],
+            slice_recv.at[i - 1],
+            x_device(i),
+        )
+        for i in (1, 3, 2)
+    ]
+    slice_keep = pltpu.make_async_copy(
+        row_in.at[:, columns_of(x)], band(share * ROWS, ROWS), local_sem.at[3]
+    )
+    slice_keep.start()
     keep.wait()
     big_copy.wait()
     for copy in core_copies:
@@ -261,30 +283,13 @@
     x_raw_down(0)
     if CHUNKS > 1:
         x_mid(1)
+    slice_keep.wait()
+    for copy in slices:
+        copy.wait_recv()
+    band_up = band_copy(0, zh * 192, 192, z_device(1))
+    band_down = band_copy(1, zh * 192, 192, z_device(-1))
     multiply(x)
 
-    @pl.when(jnp.logical_not(stays))
-    def _():
-        row_copy.wait_recv()
-
-    @pl.when(stays)
-    def _():
-        row_keep.wait()
-
-    slices = [
-        send(
-            row_in.at[:, columns_of((x + i) % 4)],
-            band(share * ROWS, ROWS),
-            slice_send.at[i - 1],
-            slice_recv.at[i - 1],
-            x_device(i),
-        )
-        for i in (1, 3, 2)
-    ]
-    slice_keep = pltpu.make_async_copy(
-        row_in.at[:, columns_of(x)], band(share * ROWS, ROWS), local_sem.at[3]
-    )
-    slice_keep.start()
     for h in range(CHUNKS):
         x_sum(h)
         if h + 1 < CHUNKS:
@@ -293,12 +298,6 @@
         if h + 2 < CHUNKS:
             x_mid(h + 2)
         if h == 0:
-            slice_keep.wait()
-            for copy in slices:
-                copy.wait_recv()
-            band_up = band_copy(0, zh * 192, 192, z_device(1))
-            band_down = band_copy(1, zh * 192, 192, z_device(-1))
-        if h == 1:
             band_up.wait_recv()
             far_up = band_copy(2, z_behind * 192, 96, z_device(1))
             band_down.wait_recv()

time: 105 us -> 98.8 us (0.941)
  Pallas kernels: 100 us -> 95 us
    pallas_call x1, Pallas kernels: 100 us -> 95 us  [body(): pl.pallas_call(kernel, out_shape=(jax.ShapeDtypeStruct((768, 64), BF16),...]
where the time goes in v6:
time: 98.8 us; the launch traced here: 98.6 us
  Pallas kernels  95 us (96%)
  local copies, waits for them, and re-layouts  2.95 us (3%)
    pallas_call x1, Pallas kernels, body(): pl.pallas_call(kernel, out_shape=(jax.ShapeDtypeStruct((768, 64), BF16),...  95 us

profile of v6, /device:TPU:1, one launch (start us, length us, event | category | flops | bytes accessed | tf_op | source)
XLA Modules:
  0.0 98.6 jit_solution(5485373378838527762)
XLA Ops:
  0.6 95.0 %shard_map.59 = (bf16[768,64]{1,0:T(8,128)(2,1)}, f32[8,64]{1,0:T(8,128)}) custom-call(s32[4,48]{1,0:T(4,128)} %lists.1, bf16[768,1536]{1,0:T(8,128)(2,1)} %inverse_hbm.1, bf16[48,1024]{1,0:T(8,128)(2,1)} %lower_hbm.1, f32[8,64]{1,0:T(8,128)} %pivot_hbm.1), custom_call_target="tpu_custom_call" | custom-call | tf_op jit(solution)/shard_map/pallas_call | solution.py:389
  95.6 1.7 %copy.6 = bf16[768,64]{0,1:T(8,128)(2,1)} copy(bf16[768,64]{1,0:T(8,128)(2,1)} %get-tuple-element.2) | data formatting | bytes 196608 | tf_op jit(solution)/shard_map/pallas_call | solution.py:389
  97.3 1.3 %copy.8 = f32[8,64]{1,0:T(8,128)} copy(f32[8,64]{1,0:T(8,128)} %get-tuple-element.7) | data formatting | bytes 4096
